TPU v7x, 32 devices: a whole 2x2x4 slice. The times are simulated.
32 devices in a mesh: groups: 2 (over y), mem: 4 (over x, core), heads: 4 (over z).
Axes of the slice: x: 2, y: 2, z: 4, core: 2. Of those that a mesh axis runs over, the one named last changes fastest.
Arguments:
- hidden: bfloat16 [32, 8192], P(('groups', 'heads')), parts along dimension 0, may hold values from -6 to 6
- norm_gain: bfloat16 [8192], P('mem'), may hold values from 0.5 to 1.5
- q_weight: bfloat16 [8192, 8192], P('mem', 'heads'), may hold values from -0.0625 to 0.0625
- k_weight: bfloat16 [8192, 1024], P('mem', 'heads'), may hold values from -1 to 1, as said below
- v_weight: bfloat16 [8192, 1024], P('mem', 'heads'), may hold values from -1 to 1, as said below
- o_weight: bfloat16 [8192, 8192], P('heads', 'mem'), may hold values from -0.0625 to 0.0625
- k_cache: bfloat16 [384, 8, 128, 128], P(('groups', 'mem'), 'heads'), parts along dimension 0, may hold values from -40 to 40, as said below
- v_cache: bfloat16 [384, 8, 128, 128], P(('groups', 'mem'), 'heads'), parts along dimension 0, may hold values from -6 to 6, as said below
- page_table: int32 [16, 24], P('groups'), parts along dimension 0, may hold values from 0 to 191, as said below
- attend_list: int32 [16, 8], P('groups'), parts along dimension 0, may hold values from 0 to 23, as said below
- lengths: int32 [16], P('groups'), parts along dimension 0, may hold values from 1409 to 3072, as said below
Outputs:
- layer_out: bfloat16 [32, 8192], P(('groups', 'heads'), 'mem'), parts along dimension 0
There are 2 independent parts, one for each index of `groups`. A program takes and returns all parts, laid end to end along the dimension named above; an argument that names none is the same for every part. Nothing has to cross between parts.
Inputs may be any that keep to these rules, and one draw needn't show every extreme that they name: `page_table`: A permutation of the pool slots 0 to 191 laid out as 8 rows of 24. The blocks named by attend_list lie at most 32 in any one range of slots m * 48 to (m + 1) * 48 - 1, and exactly 32 in some such range. `attend_list`: each row names 8 distinct blocks, all below ceil(lengths[r] / 128), among them its last block ceil(lengths[r] / 128) - 1. `lengths`: some row holds 3072 steps. `k_cache`: each key-value head is stored 1 times, the copies equal. `v_cache`: each key-value head is stored 1 times, the copies equal. `k_weight`: the 1 column blocks of each key-value head are equal. `v_weight`: the 1 column blocks of each key-value head are equal.
All inputs are finite; a program needn't handle non-finite values.
Results may differ from a plain program's by a relative error of at most 0.007.
The roundings to bfloat16 on the way count: a program that leaves them out, or rounds other values in their place, can miss the bound.
Values may be sent and summed in bfloat16 or wider, within the bound.
A program may use at most 64 MiB of HBM per device.

v0:
```python
import jax
import jax.numpy as jnp
from jax import lax
from jax.sharding import PartitionSpec as P

NEG_FILL = -1e30
EPSILON = 1e-05


def fold_owners(running, shard_piece):
    piece_peak, piece_total, piece_accum = shard_piece
    run_peak, run_total, run_accum = running
    joint_peak = jnp.maximum(run_peak, jnp.max(piece_peak, axis=0))
    piece_factor = jnp.exp(piece_peak - joint_peak[None])
    joint_total = jnp.sum(piece_total * piece_factor, axis=0)
    joint_accum = jnp.sum(piece_accum * piece_factor[..., None], axis=0)
    return (joint_peak, joint_total, joint_accum)


def shards(
    hidden,
    norm_gain,
    q_weight,
    k_weight,
    v_weight,
    o_weight,
    k_cache,
    v_cache,
    page_table,
    attend_list,
    lengths,
):
    highest = lax.Precision.HIGHEST
    mem_count = lax.axis_size("mem")
    mem_index = lax.axis_index("mem")
    feature_cols = norm_gain.shape[0]
    hidden_f = hidden.astype(jnp.float32)
    mean_sq = jnp.mean(hidden_f * hidden_f, axis=-1, keepdims=True)
    own_cols = lax.dynamic_slice_in_dim(hidden_f, mem_index * feature_cols, feature_cols, 1)
    normed = (own_cols * lax.rsqrt(mean_sq + EPSILON) * norm_gain.astype(jnp.float32)).astype(
        jnp.bfloat16
    )
    shard_piece = lax.all_gather(normed, "heads", axis=0, tiled=True)
    partial_value = jnp.concatenate(
        [
            jnp.dot(shard_piece, q_weight, preferred_element_type=jnp.float32),
            jnp.dot(shard_piece, k_weight, preferred_element_type=jnp.float32),
            jnp.dot(shard_piece, v_weight, preferred_element_type=jnp.float32),
        ],
        axis=1,
    )
    summed = lax.psum(partial_value, "mem")
    query_cols = q_weight.shape[1]
    value_cols = k_weight.shape[1]
    pool_blocks = k_cache.shape[0]
    local_kv = k_cache.shape[1]
    block_size = k_cache.shape[2]
    head_dim = k_cache.shape[3]
    row_count = lengths.shape[0]
    token_count = summed.shape[0]
    step_count = token_count // row_count
    local_heads = query_cols // head_dim
    per_kv = local_heads // local_kv
    query_count = step_count * per_kv
    scale_factor = head_dim ** (-0.5)
    queries = summed[:, :query_cols].astype(jnp.bfloat16)
    queries = queries.reshape(row_count, step_count, local_kv, per_kv, head_dim).transpose(
        0, 2, 1, 3, 4
    )
    queries = queries.reshape(row_count, local_kv, query_count, head_dim)
    new_keys = summed[:, query_cols : query_cols + value_cols].astype(jnp.bfloat16)
    new_keys = new_keys.reshape(row_count, step_count, local_kv, head_dim).transpose(0, 2, 1, 3)
    new_values = summed[:, query_cols + value_cols :].astype(jnp.bfloat16)
    new_values = new_values.reshape(row_count, step_count, local_kv, head_dim).transpose(0, 2, 1, 3)
    history = page_table.shape[1]
    pair_count = row_count * history
    block_ids = jnp.arange(history, dtype=jnp.int32)
    attended = jnp.any(attend_list[:, :, None] == block_ids[None, None, :], axis=1).reshape(
        pair_count
    )
    slot_global = mem_index * pool_blocks + jnp.arange(pool_blocks, dtype=jnp.int32)
    owner_hit = page_table.reshape(pair_count)[None, :] == slot_global[:, None]
    pair_of_slot = jnp.sum(
        jnp.where(owner_hit, jnp.arange(pair_count, dtype=jnp.int32)[None, :], 0), axis=1
    )
    slot_row = pair_of_slot // history
    slot_block = pair_of_slot % history
    slot_live = jnp.take(attended, pair_of_slot)
    capacity = 2 * row_count * attend_list.shape[1] // mem_count
    running_pos = jnp.cumsum(slot_live.astype(jnp.int32)) - 1
    picked = slot_live[None, :] & (
        running_pos[None, :] == jnp.arange(capacity, dtype=jnp.int32)[:, None]
    )
    chosen = jnp.sum(
        jnp.where(picked, jnp.arange(pool_blocks, dtype=jnp.int32)[None, :], 0), axis=1
    )
    block_keys = jnp.take(k_cache, chosen, axis=0)
    block_values = jnp.take(v_cache, chosen, axis=0)
    block_row = jnp.take(slot_row, chosen)
    block_index = jnp.take(slot_block, chosen)
    block_live = jnp.any(picked, axis=1)
    row_onehot = block_row[:, None] == jnp.arange(row_count, dtype=jnp.int32)[None, :]
    block_queries = jnp.take(queries, block_row, axis=0)
    scores = (
        jnp.einsum("cgqd,cgkd->cgqk", block_queries, block_keys, preferred_element_type=jnp.float32)
        * scale_factor
    )
    positions = block_index[:, None] * block_size + jnp.arange(block_size, dtype=jnp.int32)[None, :]
    valid = (block_live[:, None] & (positions < jnp.take(lengths, block_row)[:, None]))[
        :, None, None, :
    ]
    scores = jnp.where(valid, scores, NEG_FILL)
    block_peak = jnp.max(scores, axis=-1)
    row_peak = jnp.max(
        jnp.where(row_onehot[:, :, None, None], block_peak[:, None], NEG_FILL), axis=0
    )
    weights = jnp.where(
        valid, jnp.exp(scores - jnp.take(row_peak, block_row, axis=0)[..., None]), 0.0
    )
    weights_high = weights.astype(jnp.bfloat16)
    weights_low = (weights - weights_high.astype(jnp.float32)).astype(jnp.bfloat16)
    block_accum = jnp.einsum(
        "cgqk,cgkd->cgqd", weights_high, block_values, preferred_element_type=jnp.float32
    )
    block_accum = block_accum + jnp.einsum(
        "cgqk,cgkd->cgqd", weights_low, block_values, preferred_element_type=jnp.float32
    )
    onehot_f = row_onehot.astype(jnp.float32)
    row_sums = jnp.einsum("cr,cgq->rgq", onehot_f, jnp.sum(weights, axis=-1), precision=highest)
    row_accum = jnp.einsum("cr,cgqd->rgqd", onehot_f, block_accum, precision=highest)
    fresh_scores = (
        jnp.einsum("rgqd,rgtd->rgqt", queries, new_keys, preferred_element_type=jnp.float32)
        * scale_factor
    )
    causal = (
        jnp.arange(step_count, dtype=jnp.int32)[None, :]
        <= (jnp.arange(query_count, dtype=jnp.int32) // per_kv)[:, None]
    )
    fresh_scores = jnp.where(causal, fresh_scores, NEG_FILL)
    start_state = (
        jnp.full_like(row_peak, NEG_FILL),
        jnp.zeros_like(row_sums),
        jnp.zeros_like(row_accum),
    )
    cache_peak, cache_sum, cache_accum = fold_owners(
        start_state,
        (
            lax.all_gather(row_peak[None], "mem", axis=0, tiled=True),
            lax.all_gather(row_sums[None], "mem", axis=0, tiled=True),
            lax.all_gather(row_accum[None], "mem", axis=0, tiled=True),
        ),
    )
    final_peak = jnp.maximum(cache_peak, jnp.max(fresh_scores, axis=-1))
    carried = jnp.exp(cache_peak - final_peak)
    fresh_weights = jnp.where(causal, jnp.exp(fresh_scores - final_peak[..., None]), 0.0)
    final_sum = cache_sum * carried + jnp.sum(fresh_weights, axis=-1)
    final_accum = cache_accum * carried[..., None] + jnp.einsum(
        "rgqt,rgtd->rgqd", fresh_weights, new_values.astype(jnp.float32), precision=highest
    )
    attended_out = (final_accum / final_sum[..., None]).astype(jnp.bfloat16)
    attended_out = attended_out.reshape(
        row_count, local_kv, step_count, per_kv, head_dim
    ).transpose(0, 2, 1, 3, 4)
    attended_out = attended_out.reshape(token_count, query_cols)
    projected = lax.psum_scatter(
        jnp.dot(attended_out, o_weight, preferred_element_type=jnp.float32),
        "heads",
        scatter_dimension=0,
        tiled=True,
    )
    return projected.astype(jnp.bfloat16)


def solution(mesh):
    in_specs = (
        P(("groups", "heads"), None),
        P("mem"),
        P("mem", "heads"),
        P("mem", "heads"),
        P("mem", "heads"),
        P("heads", "mem"),
        P(("groups", "mem"), "heads", None, None),
        P(("groups", "mem"), "heads", None, None),
        P("groups", None),
        P("groups", None),
        P("groups"),
    )
    out_specs = P(("groups", "heads"), "mem")
    return jax.shard_map(shards, mesh=mesh, in_specs=in_specs, out_specs=out_specs, check_vma=False)
```

profile of v0, /device:TPU:0, one launch (start us, length us, event | category | flops | bytes accessed | tf_op | source)
XLA Modules:
  0.0 102.8 jit_solution(13370720556598059067)
XLA Ops:
  0.0 0.0 copy-start
  0.0 0.0 copy-start.1
  0.0 0.0 copy-start.6
  0.0 0.0 copy-start.7
  0.0 0.9 eq.60
  0.9 0.2 select_reduce_fusion.1
  1.2 0.8 fusion.34
  1.9 0.1 reshape.240
  2.0 0.8 gather_fusion
  2.8 0.1 copy.67
  2.9 0.1 reduce-window.8
  3.0 0.1 add_reduce_fusion
  3.1 0.1 select_reduce_fusion.2
  3.3 0.7 gather_fusion.5
  4.0 0.7 gather_fusion.4
  4.7 0.0 copy-done.1
  4.7 0.7 gather_fusion.1
  5.4 0.1 fusion.37
  5.6 0.1 fusion.38
  5.6 0.0 copy-done.6
  5.7 0.0 copy-done.7
  5.7 0.2 multiply_reduce_fusion
  5.9 0.1 fusion.35
  6.0 14.9 %all-gather.3 = bf16[4,4,2048]{2,1,0:T(4,128)(2,1)S(1)} all-gather(bf16[1,4,2048]{2,1,0:T(4,128)(2,1)S(1)} %fusion.35), channel_id=1, replica_groups=mesh['groups'=2,'mem'=4,'heads'=4] {'heads'}, dimensions={0}, use_global_device_ids=true | all-gather | bytes 81920 | tf_op jit(solution)/shard_map/all_gather | solution.py:43
  20.9 0.0 copy-start.3
  20.9 0.0 copy-start.4
  21.0 4.7 %fusion.62 = f32[16,2048]{1,0:T(8,128)S(1)} fusion(bf16[16,2048]{1,0:T(8,128)(2,1)S(1)} %reshape.322, bf16[2048,2048]{1,0:T(8,128)(2,1)} %param.17), kind=kOutput, calls=%fused_computation.117 | convolution fusion | flops 134217728 | bytes 8585216 | tf_op jit(solution)/shard_map/dot_general | solution.py:46
  25.7 0.0 copy-done.3
  25.7 0.3 fusion.63
  25.9 0.0 copy-done.4
  25.9 0.3 fusion.64
  26.2 11.7 %all-reduce.3 = bf16[16,2560]{1,0:T(8,128)(2,1)S(1)} all-reduce(f32[16,2560]{1,0:T(8,128)S(1)} %pad_maximum_fusion), channel_id=1, replica_groups=mesh['groups'=2,'mem'=4,'heads'=4] {'mem'}, use_global_device_ids=true, to_apply=%region_6.8 | all-reduce | flops 40960 | bytes 245760 | tf_op jit(solution)/shard_map/psum | solution.py:52
  38.0 1.3 %gather_fusion.2 = bf16[32,2,16,128]{3,2,1,0:T(8,128)(2,1)} fusion(bf16[8,2,16,128]{3,2,1,0:T(8,128)(2,1)S(1)} %bitcast.67, s32[1024]{0:T(1024)S(1)} %pad_clamp_fusion), kind=kCustom, calls=%fused_computation.6 | custom fusion | bytes 524416 | tf_op jit(solution)/shard_map/jit(_take)/gather | solution.py:103
  39.3 0.0 copy-done
  39.3 2.2 %gather_fusion.6 = bf16[32,2,128,128]{3,2,1,0:T(8,128)(2,1)} fusion(bf16[48,2,128,128]{3,2,1,0:T(8,128)(2,1)S(1)} %copy-done, s32[1024]{0:T(1024)S(1)} %pad_clamp_fusion.1), kind=kCustom, calls=%fused_computation.1.clone | custom fusion | bytes 4194432 | tf_op jit(solution)/shard_map/jit(_take)/gather | solution.py:97
  41.4 3.8 %fusion.60 = (f32[32,2,16]{2,1,0:T(2,128)S(1)}, f32[32,2,16,128]{3,2,1,0:T(8,128)}) fusion(bf16[32,2,128,128]{3,2,1,0:T(8,128)(2,1)} %gather_fusion.6, pred[32]{0:T(512)(128)(4,1)S(1)} %get-tuple-element.12, bf16[32,2,16,128]{3,2,1,0:T(8,128)(2,1)} %gather_fusion.2, pred[32]{0:T(512)(128)(4,1)S(1)} %get-tuple-element.14, pred[32,128]{1,0:T(8,128)(4,1)S(1)} %fusion.38), kind=kOutput, calls=%fused_computation.115 | convolution fusion | flops 35126272 | bytes 2891840 | tf_op jit(solution)/shard_map/cgqd,cgkd->cgqk/dot_general | solution.py:105
  45.2 0.1 copy.69
  45.3 0.1 select_reduce_fusion
  45.4 5.3 %all-gather.1 = f32[32,2,16]{2,1,0:T(2,128)S(1)} all-gather(f32[8,2,16]{2,1,0:T(2,128)S(1)} %select_reduce_fusion), channel_id=3, replica_groups=mesh['groups'=2,'mem'=4,'heads'=4] {'mem'}, dimensions={0}, use_global_device_ids=true | all-gather | bytes 5120 | tf_op jit(solution)/shard_map/all_gather | solution.py:148
  50.8 0.2 fusion.61
  51.1 0.6 gather_fusion.3
  51.7 0.1 broadcast_select_fusion.3
  51.8 1.4 %fusion.18 = f32[32,2,16]{2,1,0:T(2,128)S(1)} fusion(f32[32,2,16,128]{3,2,1,0:T(8,128)} %get-tuple-element.24, f32[32,2,16]{2,1,0:T(2,128)S(1)} %broadcast_select_fusion.3, pred[32,128]{1,0:T(8,128)(4,1)S(1)} %fusion.38), kind=kLoop, calls=%fused_computation.29 | loop fusion | flops 392192 | bytes 536576 | tf_op jit(solution)/shard_map/reduce_sum | solution.py:129
  53.3 0.1 fusion.31
  53.4 5.4 %all-gather.2 = f32[32,2,16]{2,0,1:T(8,128)S(1)} all-gather(f32[8,2,16]{2,0,1:T(8,128)S(1)} %fusion.31), channel_id=4, replica_groups=mesh['groups'=2,'mem'=4,'heads'=4] {'mem'}, dimensions={0}, use_global_device_ids=true | all-gather | bytes 5120 | tf_op jit(solution)/shard_map/all_gather | solution.py:149
  58.9 0.1 copy.73
  59.0 4.1 %gather_fusion.7 = bf16[32,2,128,128]{3,2,1,0:T(8,128)(2,1)} fusion(bf16[48,2,128,128]{3,2,1,0:T(8,128)(2,1)} %param.22, s32[1024]{0:T(1024)S(1)} %pad_clamp_fusion.1), kind=kCustom, calls=%fused_computation.3.clone | custom fusion | bytes 4194432 | tf_op jit(solution)/shard_map/jit(_take)/gather | solution.py:98
  63.0 0.0 copy-start.2
  63.0 0.0 copy-start.5
  63.0 2.6 %fusion.14 = f32[32,2,16,128]{3,2,1,0:T(8,128)S(1)} fusion(bf16[32,2,128,128]{3,2,1,0:T(8,128)(2,1)} %gather_fusion.7, pred[32]{0:T(512)(128)(4,1)S(1)} %get-tuple-element.12, f32[32,2,16,128]{3,2,1,0:T(8,128)} %get-tuple-element.24, f32[32,2,16]{2,1,0:T(2,128)S(1)} %broadcast_select_fusion.3, pred[32,128]{1,0:T(8,128)(4,1)S(1)} %fusion.38), kind=kOutput, calls=%fused_computation.22 | convolution fusion | flops 34996224 | bytes 3153952 | tf_op jit(solution)/shard_map/cgqk,cgkd->cgqd/dot_general | solution.py:122
  65.6 0.0 copy-done.2
  65.6 0.0 copy-done.5
  65.6 0.7 convolution_add_fusion
  66.4 0.6 fusion.16
  67.0 7.4 %all-gather = f32[32,2,16,128]{3,0,2,1:T(8,128)S(1)} all-gather(f32[8,2,16,128]{3,0,2,1:T(8,128)S(1)} %fusion.16), channel_id=2, replica_groups=mesh['groups'=2,'mem'=4,'heads'=4] {'mem'}, dimensions={0}, use_global_device_ids=true | all-gather | bytes 655360 | tf_op jit(solution)/shard_map/all_gather | solution.py:150
  74.4 0.2 fusion.15
  74.6 0.3 fusion.11
  75.0 0.0 copy-start.8
  75.0 4.6 %fusion.65 = f32[16,2048]{1,0:T(8,128)S(1)} fusion(bf16[16,2048]{1,0:T(8,128)(2,1)S(1)} %reshape.246, bf16[2048,2048]{1,0:T(8,128)(2,1)} %param.20), kind=kOutput, calls=%fused_computation.120 | convolution fusion | flops 134217728 | bytes 8585216 | tf_op jit(solution)/shard_map/dot_general | solution.py:166
  79.6 21.4 %all-reduce.4 = bf16[16,2048]{1,0:T(8,128)(2,1)S(1)} all-reduce(f32[16,2048]{1,0:T(8,128)S(1)} %fusion.65), channel_id=5, replica_groups=mesh['groups'=2,'mem'=4,'heads'=4] {'heads'}, use_global_device_ids=true, to_apply=%region_15.18.clone | all-reduce | flops 32768 | bytes 196608
  101.0 0.0 copy-done.8
  101.0 0.6 dynamic-slice
  102.2 0.6 dynamic-slice_convert_fusion
  (34 shorter events, 0.4 us)
Async XLA Ops:
  0.0 39.3 %copy-start = (bf16[48,2,128,128]{3,2,1,0:T(8,128)(2,1)S(1)}, bf16[48,2,128,128]{3,2,1,0:T(8,128)(2,1)}, u32[]{:S(2)}) copy-start(bf16[48,2,128,128]{3,2,1,0:T(8,128)(2,1)} %param.21) | copy-start | bytes 9437188
  0.0 4.7 %copy-start.1 = (s32[8]{0:T(128)S(1)}, s32[8]{0:T(128)}, u32[]{:S(2)}) copy-start(s32[8]{0:T(128)} %param.25) | copy-start | bytes 100
  0.0 5.6 %copy-start.6 = (bf16[4,8192]{1,0:T(4,128)(2,1)S(1)}, bf16[4,8192]{1,0:T(4,128)(2,1)}, u32[]{:S(2)}) copy-start(bf16[4,8192]{1,0:T(4,128)(2,1)} %param.15) | copy-start | bytes 196612
  0.0 5.7 %copy-start.7 = (bf16[2048]{0:T(1024)(128)(2,1)S(1)}, bf16[2048]{0:T(1024)(128)(2,1)}, u32[]{:S(2)}) copy-start(bf16[2048]{0:T(1024)(128)(2,1)} %param.16) | copy-start | bytes 12292
  20.9 4.7 %copy-start.3 = (bf16[2048,256]{1,0:T(8,128)(2,1)S(1)}, bf16[2048,256]{1,0:T(8,128)(2,1)}, u32[]{:S(2)}) copy-start(bf16[2048,256]{1,0:T(8,128)(2,1)} %param.18) | copy-start | bytes 3145732
  20.9 5.0 %copy-start.4 = (bf16[2048,256]{1,0:T(8,128)(2,1)S(1)}, bf16[2048,256]{1,0:T(8,128)(2,1)}, u32[]{:S(2)}) copy-start(bf16[2048,256]{1,0:T(8,128)(2,1)} %param.19) | copy-start | bytes 3145732
  63.0 2.6 %copy-start.2 = (bf16[32,2,128,128]{3,2,1,0:T(8,128)(2,1)S(1)}, bf16[32,2,128,128]{3,2,1,0:T(8,128)(2,1)}, u32[]{:S(2)}) copy-start(bf16[32,2,128,128]{3,2,1,0:T(8,128)(2,1)} %gather_fusion.7) | copy-start | bytes 6291460
  63.0 2.6 %copy-start.5 = (f32[32,2,16,128]{3,2,1,0:T(8,128)S(1)}, f32[32,2,16,128]{3,2,1,0:T(8,128)}, u32[]{:S(2)}) copy-start(f32[32,2,16,128]{3,2,1,0:T(8,128)} %get-tuple-element.24) | copy-start | bytes 1572868
  75.0 26.0 %copy-start.8 = (u32[32]{0:T(128)S(1)}, u32[32]{0:T(128)}, u32[]{:S(2)}) copy-start(u32[32]{0:T(128)} %constant.151) | copy-start | bytes 388
where the time goes:
time: 103 us
  blocking collectives  66.2 us (64%)
  matrix products  18.2 us (18%)
  local copies, waits for them, and re-layouts  13.6 us (13%)
  other arithmetic  3.86 us (4%)
    unnamed x1, blocking collectives  21.4 us
    all_gather x1, blocking collectives, shards(): shard_piece = lax.all_gather(normed, 'heads', axis=0, tiled=True)  14.9 us
    psum x1, blocking collectives, shards(): summed = lax.psum(partial_value, 'mem')  11.7 us
    all_gather x1, blocking collectives, shards(): lax.all_gather(row_accum[None], 'mem', axis=0, tiled=True)  7.38 us
    all_gather x1, blocking collectives, shards(): lax.all_gather(row_sums[None], 'mem', axis=0, tiled=True)  5.43 us
    all_gather x1, blocking collectives, shards(): lax.all_gather(row_peak[None], 'mem', axis=0, tiled=True)  5.32 us
    dot_general x1, matrix products, shards(): jnp.dot(shard_piece, q_weight, preferred_element_type=jnp.float32)  4.72 us
    dot_general x1, matrix products, shards(): jnp.dot(attended_out, o_weight, preferred_element_type=jnp.float32)  4.58 us

commit v1 on v0

v1 whole, which is shorter than its diff:
```python
import functools

import jax
import jax.numpy as jnp
from jax import lax
from jax.experimental import pallas as pl
from jax.experimental.pallas import tpu as pltpu
from jax.sharding import PartitionSpec as P

MESH = pl.DeviceIdType.MESH
NEG_FILL = -1e30
EPSILON = 1e-05
PIECES = 4
F32 = jnp.float32
BF16 = jnp.bfloat16


def layer_kernel(
    mem_count,
    head_count,
    chunks,
    page_ref,
    attend_ref,
    length_ref,
    hidden_ref,
    gain_ref,
    wq_hbm,
    wk_hbm,
    wv_hbm,
    wo_hbm,
    kc_hbm,
    vc_hbm,
    out_ref,
    wq,
    wk,
    wv,
    wo,
    kc,
    vc,
    norm_buf,
    part,
    part_in,
    own_heads,
    heads_all,
    row_queries,
    accum,
    accum_in,
    stat_in,
    own_att,
    att_all,
    proj,
    proj_in,
    load_sem,
    norm_send,
    norm_recv,
    part_send,
    part_recv,
    heads_send,
    heads_recv,
    accum_send,
    accum_recv,
    stat_send,
    stat_recv,
    att_send,
    att_recv,
    proj_send,
    proj_recv,
):
    mem = lax.axis_index("mem")
    head = lax.axis_index("heads")
    row_count, sel = attend_ref.shape
    features = wq.shape[0]
    q_cols, kv_cols = wq.shape[1], wk.shape[1]
    pool, local_kv, block, dim = kc.shape
    tokens = accum.shape[0]
    steps = tokens // row_count
    own_tokens = tokens // mem_count
    head_tokens = tokens // head_count
    local_heads = q_cols // dim
    per_kv = local_heads // local_kv
    queries = steps * per_kv
    scale = dim ** (-0.5)

    def mem_peer(k):
        return lax.rem(mem + k, mem_count)

    def mem_source(k):
        return lax.rem(mem + mem_count - k, mem_count)

    def head_peer(k):
        return lax.rem(head + k, head_count)

    def head_source(k):
        return lax.rem(head + head_count - k, head_count)

    loads = []
    for which, (source, target) in enumerate(
        ((wk_hbm, wk), (wv_hbm, wv), (wq_hbm, wq), (kc_hbm, kc), (vc_hbm, vc), (wo_hbm, wo))
    ):
        rows = source.shape[0] // PIECES
        group = []
        for piece in range(PIECES):
            view = pl.ds(piece * rows, rows)
            copy = pltpu.make_async_copy(
                source.at[view], target.at[view], load_sem.at[which, piece]
            )
            copy.start()
            group.append(copy)
        loads.append(group)

    def arrive(which):
        for copy in loads[which]:
            copy.wait()

    barrier = pltpu.get_barrier_semaphore()
    for k in range(1, mem_count):
        pl.semaphore_signal(barrier, inc=1, device_id={"mem": mem_peer(k)}, device_id_type=MESH)
    for k in range(1, head_count):
        pl.semaphore_signal(barrier, inc=1, device_id={"heads": head_peer(k)}, device_id_type=MESH)

    hidden = hidden_ref[...].astype(F32)
    mean_sq = jnp.mean(hidden * hidden, axis=-1, keepdims=True)
    own = hidden_ref[:, pl.ds(pl.multiple_of(mem * features, 128), features)].astype(F32)
    normed = own * lax.rsqrt(mean_sq + EPSILON) * gain_ref[...].astype(F32)
    norm_buf[head] = normed.astype(BF16)

    pl.semaphore_wait(barrier, mem_count + head_count - 2)

    def norm_copy(k, slot):
        return pltpu.make_async_remote_copy(
            norm_buf.at[slot],
            norm_buf.at[slot],
            norm_send.at[k],
            norm_recv.at[k],
            device_id={"heads": head_peer(k)},
            device_id_type=MESH,
        )

    for k in range(head_count - 1, 0, -1):
        norm_copy(k, head).start()
    for k in range(1, head_count):
        norm_copy(k, head_source(k)).wait_recv()
    lhs = jnp.concatenate([norm_buf[i].astype(F32) for i in range(head_count)], axis=0).astype(BF16)

    def part_copy(index, start, width, k, target, slot):
        view = pl.ds(start, width)
        return pltpu.make_async_remote_copy(
            part.at[target, :, view],
            part_in.at[slot, :, view],
            part_send.at[index, k],
            part_recv.at[index, k],
            device_id={"mem": mem_peer(k)},
            device_id_type=MESH,
        )

    chunk = q_cols // chunks
    pieces = [(index, index * chunk, chunk) for index in range(chunks)]
    pieces.append((chunks, q_cols, 2 * kv_cols))

    arrive(0)
    arrive(1)
    fresh = jnp.concatenate(
        [
            jnp.dot(lhs, wk[...], preferred_element_type=F32),
            jnp.dot(lhs, wv[...], preferred_element_type=F32),
        ],
        axis=1,
    )
    for owner in range(mem_count):
        part[owner, :, q_cols:] = fresh[owner * own_tokens : (owner + 1) * own_tokens]
    for k in range(1, mem_count):
        part_copy(chunks, q_cols, 2 * kv_cols, k, mem_peer(k), mem).start()
    arrive(2)
    for index, start, width in pieces[:-1]:
        view = pl.ds(start, width)
        value = jnp.dot(lhs, wq[:, view], preferred_element_type=F32)
        for owner in range(mem_count):
            part[owner, :, view] = value[owner * own_tokens : (owner + 1) * own_tokens]
        for k in range(1, mem_count):
            part_copy(index, start, width, k, mem_peer(k), mem).start()

    total = part[mem]
    for k in range(1, mem_count):
        for index, start, width in pieces:
            part_copy(index, start, width, k, mem_peer(k), mem_source(k)).wait_recv()
        total = total + part_in[mem_source(k)]
    all_heads = local_heads + 2 * local_kv
    for h in range(all_heads):
        own_heads[:, h, :] = total[:, h * dim : (h + 1) * dim]
    heads_all[mem] = own_heads[...].astype(BF16)

    def heads_copy(k, slot):
        return pltpu.make_async_remote_copy(
            heads_all.at[slot],
            heads_all.at[slot],
            heads_send.at[k],
            heads_recv.at[k],
            device_id={"mem": mem_peer(k)},
            device_id_type=MESH,
        )

    for k in range(1, mem_count):
        heads_copy(k, mem).start()
    for k in range(1, mem_count):
        heads_copy(k, mem_source(k)).wait_recv()

    for r in range(row_count):
        token_heads = []
        for s in range(steps):
            t = r * steps + s
            token_heads.append(heads_all[t // own_tokens, t % own_tokens].astype(F32))
        for g in range(local_kv):
            row_queries[r, g] = jnp.concatenate(
                [value[g * per_kv : (g + 1) * per_kv] for value in token_heads], axis=0
            ).astype(BF16)

    arrive(3)
    arrive(4)
    lane = lax.broadcasted_iota(jnp.int32, (queries, dim), 1)
    key_lane = lax.broadcasted_iota(jnp.int32, (queries, block), 1)

    def attend_row(r, stat):
        slots, counts = [], []
        for j in range(sel):
            named = attend_ref[r, j]
            slot = page_ref[r, named] - mem * pool
            local = (slot >= 0) & (slot < pool)
            slots.append(jnp.clip(slot, 0, pool - 1))
            counts.append(jnp.where(local, length_ref[r] - named * block, 0))
        for g in range(local_kv):
            keys = jnp.concatenate([kc[slot, g] for slot in slots], axis=0)
            scores = lax.dot_general(
                row_queries[r, g],
                keys,
                (((1,), (1,)), ((), ())),
                preferred_element_type=F32,
            )
            valid = [key_lane < count for count in counts]
            kept = [
                jnp.where(valid[j], scores[:, j * block : (j + 1) * block] * scale, NEG_FILL)
                for j in range(sel)
            ]
            peak = jnp.max(functools.reduce(jnp.maximum, kept), axis=1, keepdims=True)
            weights = [jnp.where(valid[j], jnp.exp(kept[j] - peak), 0.0) for j in range(sel)]
            mass = jnp.sum(functools.reduce(jnp.add, weights), axis=1, keepdims=True)
            high = [w.astype(BF16) for w in weights]
            low = [(w - h.astype(F32)).astype(BF16) for w, h in zip(weights, high)]
            both = jnp.concatenate(
                [jnp.concatenate(high, axis=1), jnp.concatenate(low, axis=1)], axis=0
            )
            values = jnp.concatenate([vc[slot, g] for slot in slots], axis=0)
            mixed = jnp.dot(both, values, preferred_element_type=F32)
            mixed = mixed[:queries] + mixed[queries:]
            for s in range(steps):
                accum[r * steps + s, g] = mixed[s * per_kv : (s + 1) * per_kv]
            spot = r * local_kv + g
            stat = jnp.where(lane == spot, peak, stat)
            stat = jnp.where(lane == spot + row_count * local_kv, mass, stat)
        return stat

    stat = lax.fori_loop(0, row_count, attend_row, jnp.zeros((queries, dim), F32))
    for s in range(steps):
        stat_in[mem, s] = stat[s * per_kv : (s + 1) * per_kv]

    def stat_copy(k, slot):
        return pltpu.make_async_remote_copy(
            stat_in.at[slot],
            stat_in.at[slot],
            stat_send.at[k],
            stat_recv.at[k],
            device_id={"mem": mem_peer(k)},
            device_id_type=MESH,
        )

    def accum_copy(k, target, slot):
        return pltpu.make_async_remote_copy(
            accum.at[pl.ds(target * own_tokens, own_tokens)],
            accum_in.at[slot],
            accum_send.at[k],
            accum_recv.at[k],
            device_id={"mem": mem_peer(k)},
            device_id_type=MESH,
        )

    for k in range(1, mem_count):
        stat_copy(k, mem).start()
        accum_copy(k, mem_peer(k), mem).start()
    accum_in[mem] = accum[pl.ds(mem * own_tokens, own_tokens)]

    fresh_parts = []
    stat_lane = lax.broadcasted_iota(jnp.int32, (per_kv, dim), 1)
    for tl in range(own_tokens):
        t = mem * own_tokens + tl
        r, s = t // steps, t % steps
        own_query = heads_all[mem, tl].astype(F32)
        row_heads = []
        for u in range(steps):
            tu = r * steps + u
            row_heads.append(heads_all[tu // own_tokens, tu % own_tokens].astype(F32))
        for g in range(local_kv):
            query = own_query[g * per_kv : (g + 1) * per_kv]
            scores, new_values = [], []
            for u in range(steps):
                at = local_heads + g
                key = row_heads[u][at : at + 1]
                at = local_heads + local_kv + g
                new_values.append(row_heads[u][at : at + 1])
                score = jnp.sum(query * key, axis=1, keepdims=True) * scale
                seen = jnp.broadcast_to(s, (per_kv, 1)) >= u
                scores.append(jnp.where(seen, score, NEG_FILL))
            top = functools.reduce(jnp.maximum, scores)
            fresh_parts.append((r, s, scores, top, new_values))

    for k in range(1, mem_count):
        stat_copy(k, mem_source(k)).wait_recv()
        accum_copy(k, mem_peer(k), mem_source(k)).wait_recv()

    for tl in range(own_tokens):
        for g in range(local_kv):
            r, s, scores, top, new_values = fresh_parts[tl * local_kv + g]
            spot = r * local_kv + g
            stats = [stat_in[d, s] for d in range(mem_count)]
            peaks = [
                jnp.sum(jnp.where(stat_lane == spot, x, 0.0), axis=1, keepdims=True) for x in stats
            ]
            masses = [
                jnp.sum(
                    jnp.where(stat_lane == spot + row_count * local_kv, x, 0.0),
                    axis=1,
                    keepdims=True,
                )
                for x in stats
            ]
            peak = functools.reduce(jnp.maximum, peaks, top)
            mass = jnp.zeros((per_kv, 1), F32)
            mixed = jnp.zeros((per_kv, dim), F32)
            for u in range(steps):
                weight = jnp.exp(scores[u] - peak)
                mass = mass + weight
                mixed = mixed + weight * new_values[u]
            for d in range(mem_count):
                factor = jnp.exp(peaks[d] - peak)
                mass = mass + masses[d] * factor
                mixed = mixed + accum_in[d, tl, g] * factor
            own_att[tl, g * per_kv : (g + 1) * per_kv, :] = mixed / mass
    att_all[mem] = jnp.concatenate([own_att[:, h, :] for h in range(local_heads)], axis=1).astype(
        BF16
    )

    def att_copy(k, slot):
        return pltpu.make_async_remote_copy(
            att_all.at[slot],
            att_all.at[slot],
            att_send.at[k],
            att_recv.at[k],
            device_id={"mem": mem_peer(k)},
            device_id_type=MESH,
        )

    for k in range(1, mem_count):
        att_copy(k, mem).start()
    for k in range(1, mem_count):
        att_copy(k, mem_source(k)).wait_recv()
    lhs = jnp.concatenate([att_all[i].astype(F32) for i in range(mem_count)], axis=0).astype(BF16)

    def proj_copy(index, width, k, target, slot):
        view = pl.ds(index * width, width)
        return pltpu.make_async_remote_copy(
            proj.at[target, :, view],
            proj_in.at[slot, :, view],
            proj_send.at[index, k],
            proj_recv.at[index, k],
            device_id={"heads": head_peer(k)},
            device_id_type=MESH,
        )

    arrive(5)
    width = wo.shape[1] // chunks
    for index in range(chunks):
        view = pl.ds(index * width, width)
        value = jnp.dot(lhs, wo[:, view], preferred_element_type=F32)
        for owner in range(head_count):
            proj[owner, :, view] = value[owner * head_tokens : (owner + 1) * head_tokens]
        for k in range(head_count - 1, 0, -1):
            proj_copy(index, width, k, head_peer(k), head).start()
    total = proj[head]
    for k in range(1, head_count):
        for index in range(chunks):
            proj_copy(index, width, k, head_peer(k), head_source(k)).wait_recv()
        total = total + proj_in[head_source(k)]
    out_ref[...] = total.astype(BF16)

    for k in range(1, head_count):
        norm_copy(k, head).wait_send()
        for index in range(chunks):
            proj_copy(index, width, k, head_peer(k), head).wait_send()
    for k in range(1, mem_count):
        for index, start, size in pieces:
            part_copy(index, start, size, k, mem_peer(k), mem).wait_send()
        heads_copy(k, mem).wait_send()
        stat_copy(k, mem).wait_send()
        accum_copy(k, mem_peer(k), mem).wait_send()
        att_copy(k, mem).wait_send()


def shards(
    hidden,
    norm_gain,
    q_weight,
    k_weight,
    v_weight,
    o_weight,
    k_cache,
    v_cache,
    page_table,
    attend_list,
    lengths,
):
    mem_count = lax.axis_size("mem")
    head_count = lax.axis_size("heads")
    features, q_cols = q_weight.shape
    kv_cols = k_weight.shape[1]
    _, local_kv, _, dim = k_cache.shape
    row_count = lengths.shape[0]
    tokens = hidden.shape[0] * head_count
    steps = tokens // row_count
    own_tokens = tokens // mem_count
    head_tokens = hidden.shape[0]
    local_heads = q_cols // dim
    per_kv = local_heads // local_kv
    out_cols = o_weight.shape[1]
    chunks = 4
    smem = pl.BlockSpec(memory_space=pltpu.SMEM)
    vmem = pl.BlockSpec(memory_space=pltpu.VMEM)
    hbm = pl.BlockSpec(memory_space=pl.ANY)
    dma = pltpu.SemaphoreType.DMA
    total_heads = local_heads + 2 * local_kv
    return pl.pallas_call(
        functools.partial(layer_kernel, mem_count, head_count, chunks),
        out_shape=jax.ShapeDtypeStruct((head_tokens, out_cols), BF16),
        in_specs=[smem] * 3 + [vmem] * 2 + [hbm] * 6,
        out_specs=vmem,
        scratch_shapes=[
            pltpu.VMEM(q_weight.shape, BF16),
            pltpu.VMEM(k_weight.shape, BF16),
            pltpu.VMEM(v_weight.shape, BF16),
            pltpu.VMEM(o_weight.shape, BF16),
            pltpu.VMEM(k_cache.shape, BF16),
            pltpu.VMEM(v_cache.shape, BF16),
            pltpu.VMEM((head_count, head_tokens, features), BF16),
            pltpu.VMEM((mem_count, own_tokens, q_cols + 2 * kv_cols), F32),
            pltpu.VMEM((mem_count, own_tokens, q_cols + 2 * kv_cols), F32),
            pltpu.VMEM((own_tokens, total_heads, dim), F32),
            pltpu.VMEM((mem_count, own_tokens, total_heads, dim), BF16),
            pltpu.VMEM((row_count, local_kv, steps * per_kv, dim), BF16),
            pltpu.VMEM((tokens, local_kv, per_kv, dim), F32),
            pltpu.VMEM((mem_count, own_tokens, local_kv, per_kv, dim), F32),
            pltpu.VMEM((mem_count, steps, per_kv, dim), F32),
            pltpu.VMEM((own_tokens, local_heads, dim), F32),
            pltpu.VMEM((mem_count, own_tokens, q_cols), BF16),
            pltpu.VMEM((head_count, head_tokens, out_cols), F32),
            pltpu.VMEM((head_count, head_tokens, out_cols), F32),
            dma((6, PIECES)),
            dma((head_count,)),
            dma((head_count,)),
            dma((chunks + 1, mem_count)),
            dma((chunks + 1, mem_count)),
            dma((mem_count,)),
            dma((mem_count,)),
            dma((mem_count,)),
            dma((mem_count,)),
            dma((mem_count,)),
            dma((mem_count,)),
            dma((mem_count,)),
            dma((mem_count,)),
            dma((chunks, head_count)),
            dma((chunks, head_count)),
        ],
        compiler_params=pltpu.CompilerParams(
            collective_id=0, has_side_effects=True, vmem_limit_bytes=60 * 1024 * 1024
        ),
    )(
        page_table,
        attend_list,
        lengths,
        hidden,
        norm_gain.reshape(1, -1),
        q_weight,
        k_weight,
        v_weight,
        o_weight,
        k_cache,
        v_cache,
    )


def solution(mesh):
    in_specs = (
        P(("groups", "heads"), None),
        P("mem"),
        P("mem", "heads"),
        P("mem", "heads"),
        P("mem", "heads"),
        P("heads", "mem"),
        P(("groups", "mem"), "heads", None, None),
        P(("groups", "mem"), "heads", None, None),
        P("groups", None),
        P("groups", None),
        P("groups"),
    )
    out_specs = P(("groups", "heads"), "mem")
    return jax.shard_map(shards, mesh=mesh, in_specs=in_specs, out_specs=out_specs, check_vma=False)
```

time: 103 us -> 39.7 us (0.39)
  blocking collectives: 66.2 us -> 0 us
  Pallas kernels: 0 us -> 36.8 us
  matrix products: 18.2 us -> 0 us
  local copies, waits for them, and re-layouts: 13.6 us -> 2.62 us
  other arithmetic: 3.86 us -> 0 us
    pallas_call x0 -> x1, Pallas kernels: none -> 36.8 us  [shards(): pl.pallas_call(functools.partial(layer_kernel, mem_count, head_count, chu...]
    all_gather x4 -> x0, blocking collectives: 33.1 us -> none  [the longest x1 14.9 us: shards(): shard_piece = lax.all_gather(normed, 'heads', axis=0, tiled=True)]
    unnamed x1 -> x0, blocking collectives: 21.4 us -> none
    dot_general x11 -> x0, matrix products: 18.2 us -> none  [the longest x1 4.72 us: shards(): jnp.dot(shard_piece, q_weight, preferred_element_type=jnp.float32)]
    psum x1 -> x0, blocking collectives: 11.7 us -> none  [shards(): summed = lax.psum(partial_value, 'mem')]
    gather x8 -> x0, local copies, waits for them, and re-layouts: 11 us -> none  [the longest x1 4.06 us: shards(): block_values = jnp.take(v_cache, chosen, axis=0)]
    reduce_sum x7 -> x0, other arithmetic: 2.19 us -> none  [the longest x1 1.44 us: shards(): jnp.sum(weights, axis=-1)]
    reshape x5 -> x1, local copies, waits for them, and re-layouts: 0.15 us -> 1.29 us  [shards(): norm_gain.reshape(1, -1)]
where the time goes in v1:
time: 39.7 us; the launch traced here: 39.4 us
  Pallas kernels  36.8 us (93%)
  local copies, waits for them, and re-layouts  2.62 us (7%)
    pallas_call x1, Pallas kernels, shards(): pl.pallas_call(functools.partial(layer_kernel, mem_count, head_count, chu...  36.8 us
    unnamed x1, local copies, waits for them, and re-layouts  1.33 us
    reshape x1, local copies, waits for them, and re-layouts, shards(): norm_gain.reshape(1, -1)  1.29 us

profile of v1, /device:TPU:0, one launch (start us, length us, event | category | flops | bytes accessed | tf_op | source)
XLA Modules:
  0.0 39.4 jit_solution(6999444822233652055)
XLA Ops:
  0.0 1.3 %reshape.3.gain_ref = bf16[1,2048]{1,0:T(2,128)(2,1)} reshape(bf16[2048]{0:T(1024)(128)(2,1)} %param.12) | data formatting | bytes 8192 | tf_op jit(solution)/shard_map/reshape | solution.py:487
  1.3 36.8 %shard_map.109 = bf16[4,2048]{1,0:T(4,128)(2,1)} custom-call(s32[8,24]{1,0:T(8,128)} %page_ref.1, s32[8,8]{1,0:T(8,128)} %attend_ref.1, s32[8]{0:T(128)} %length_ref.1, bf16[4,8192]{1,0:T(4,128)(2,1)} %hidden_ref.1, bf16[1,2048]{1,0:T(2,128)(2,1)} %reshape.3.gain_ref, bf16[2048,2048]{1,0:T(8,128)(2,1)} %wq_hbm.1, bf16[2048,256]{1,0:T(8,128)(2,1)} %wk_hbm.1, ...), custom_call_target="tpu_custom_call" | custom-call | tf_op jit(solution)/shard_map/pallas_call | solution.py:438
  38.1 1.3 %copy.13 = bf16[4,2048]{1,0:T(4,128)(2,1)} copy(bf16[4,2048]{1,0:T(4,128)(2,1)} %shard_map.109) | data formatting | bytes 32768

commit v2 on v1

--- a/solution.py
+++ b/solution.py
@@ -104,14 +104,19 @@
             copy = pltpu.make_async_copy(
                 source.at[view], target.at[view], load_sem.at[which, piece]
             )
-            copy.start()
             group.append(copy)
         loads.append(group)
+
+    def begin(which):
+        for copy in loads[which]:
+            copy.start()
 
     def arrive(which):
         for copy in loads[which]:
             copy.wait()
 
+    for which in range(3):
+        begin(which)
     barrier = pltpu.get_barrier_semaphore()
     for k in range(1, mem_count):
         pl.semaphore_signal(barrier, inc=1, device_id={"mem": mem_peer(k)}, device_id_type=MESH)
@@ -121,7 +126,7 @@
     hidden = hidden_ref[...].astype(F32)
     mean_sq = jnp.mean(hidden * hidden, axis=-1, keepdims=True)
     own = hidden_ref[:, pl.ds(pl.multiple_of(mem * features, 128), features)].astype(F32)
-    normed = own * lax.rsqrt(mean_sq + EPSILON) * gain_ref[...].astype(F32)
+    normed = own * lax.rsqrt(mean_sq + EPSILON) * gain_ref[...].astype(F32).reshape(1, features)
     norm_buf[head] = normed.astype(BF16)
 
     pl.semaphore_wait(barrier, mem_count + head_count - 2)
@@ -171,6 +176,8 @@
     for k in range(1, mem_count):
         part_copy(chunks, q_cols, 2 * kv_cols, k, mem_peer(k), mem).start()
     arrive(2)
+    for which in range(3, 6):
+        begin(which)
     for index, start, width in pieces[:-1]:
         view = pl.ds(start, width)
         value = jnp.dot(lhs, wq[:, view], preferred_element_type=F32)
@@ -258,7 +265,36 @@
             stat = jnp.where(lane == spot + row_count * local_kv, mass, stat)
         return stat
 
-    stat = lax.fori_loop(0, row_count, attend_row, jnp.zeros((queries, dim), F32))
+    def accum_copy(k, target, slot):
+        return pltpu.make_async_remote_copy(
+            accum.at[pl.ds(target * own_tokens, own_tokens)],
+            accum_in.at[slot],
+            accum_send.at[k],
+            accum_recv.at[k],
+            device_id={"mem": mem_peer(k)},
+            device_id_type=MESH,
+        )
+
+    stat = jnp.zeros((queries, dim), F32)
+    if own_tokens % steps == 0:
+        own_rows = own_tokens // steps
+
+        def attend_owner(b, stat):
+            owner = mem_peer(b + 1)
+            for row in range(own_rows):
+                stat = attend_row(owner * own_rows + row, stat)
+
+            @pl.when(b < mem_count - 1)
+            def _():
+                accum_copy(b + 1, owner, mem).start()
+
+            return stat
+
+        stat = lax.fori_loop(0, mem_count, attend_owner, stat)
+    else:
+        stat = lax.fori_loop(0, row_count, attend_row, stat)
+        for k in range(1, mem_count):
+            accum_copy(k, mem_peer(k), mem).start()
     for s in range(steps):
         stat_in[mem, s] = stat[s * per_kv : (s + 1) * per_kv]
 
@@ -272,19 +308,8 @@
             device_id_type=MESH,
         )
 
-    def accum_copy(k, target, slot):
-        return pltpu.make_async_remote_copy(
-            accum.at[pl.ds(target * own_tokens, own_tokens)],
-            accum_in.at[slot],
-            accum_send.at[k],
-            accum_recv.at[k],
-            device_id={"mem": mem_peer(k)},
-            device_id_type=MESH,
-        )
-
     for k in range(1, mem_count):
         stat_copy(k, mem).start()
-        accum_copy(k, mem_peer(k), mem).start()
     accum_in[mem] = accum[pl.ds(mem * own_tokens, own_tokens)]
 
     fresh_parts = []
@@ -484,7 +509,7 @@
         attend_list,
         lengths,
         hidden,
-        norm_gain.reshape(1, -1),
+        norm_gain,
         q_weight,
         k_weight,
         v_weight,

time: 39.7 us -> 37.3 us (0.940)
  local copies, waits for them, and re-layouts: 2.62 us -> 1.33 us
  Pallas kernels: 36.8 us -> 35.7 us
    reshape x1 -> x0, local copies, waits for them, and re-layouts: 1.29 us -> none  [shards(): norm_gain.reshape(1, -1)]
    pallas_call x1, Pallas kernels: 36.8 us -> 35.7 us  [shards(): pl.pallas_call(functools.partial(layer_kernel, mem_count, head_count, chu...]
where the time goes in v2:
time: 37.3 us; the launch traced here: 37 us
  Pallas kernels  35.7 us (96%)
  local copies, waits for them, and re-layouts  1.33 us (4%)
    pallas_call x1, Pallas kernels, shards(): pl.pallas_call(functools.partial(layer_kernel, mem_count, head_count, chu...  35.7 us
    unnamed x1, local copies, waits for them, and re-layouts  1.33 us

profile of v2, /device:TPU:0, one launch (start us, length us, event | category | flops | bytes accessed | tf_op | source)
XLA Modules:
  0.0 37.0 jit_solution(6988470237327698053)
XLA Ops:
  0.0 35.7 %shard_map.109 = bf16[4,2048]{1,0:T(4,128)(2,1)} custom-call(s32[8,24]{1,0:T(8,128)} %page_ref.1, s32[8,8]{1,0:T(8,128)} %attend_ref.1, s32[8]{0:T(128)} %length_ref.1, bf16[4,8192]{1,0:T(4,128)(2,1)} %hidden_ref.1, bf16[2048]{0:T(1024)(128)(2,1)} %gain_ref.1, bf16[2048,2048]{1,0:T(8,128)(2,1)} %wq_hbm.1, bf16[2048,256]{1,0:T(8,128)(2,1)} %wk_hbm.1, ...), custom_call_target="tpu_custom_call" | custom-call | tf_op jit(solution)/shard_map/pallas_call | solution.py:463
  35.7 1.3 %copy.13 = bf16[4,2048]{1,0:T(4,128)(2,1)} copy(bf16[4,2048]{1,0:T(4,128)(2,1)} %shard_map.109) | data formatting | bytes 32768

commit v3 on v2

--- a/solution.py
+++ b/solution.py
@@ -226,37 +226,54 @@
     lane = lax.broadcasted_iota(jnp.int32, (queries, dim), 1)
     key_lane = lax.broadcasted_iota(jnp.int32, (queries, block), 1)
 
-    def attend_row(r, stat):
-        slots, counts = [], []
-        for j in range(sel):
-            named = attend_ref[r, j]
-            slot = page_ref[r, named] - mem * pool
-            local = (slot >= 0) & (slot < pool)
-            slots.append(jnp.clip(slot, 0, pool - 1))
-            counts.append(jnp.where(local, length_ref[r] - named * block, 0))
-        for g in range(local_kv):
-            keys = jnp.concatenate([kc[slot, g] for slot in slots], axis=0)
-            scores = lax.dot_general(
+    def attend_rows(rows, stat):
+        jobs, masks, slot_lists = [], {}, {}
+        for n, r in enumerate(rows):
+            slots, masks[n] = [], []
+            for j in range(sel):
+                named = attend_ref[r, j]
+                slot = page_ref[r, named] - mem * pool
+                local = (slot >= 0) & (slot < pool)
+                slots.append(jnp.clip(slot, 0, pool - 1))
+                masks[n].append(key_lane < jnp.where(local, length_ref[r] - named * block, 0))
+            slot_lists[n] = slots
+            jobs.extend((n, r, g) for g in range(local_kv))
+        raw = [
+            lax.dot_general(
                 row_queries[r, g],
-                keys,
+                jnp.concatenate([kc[slot, g] for slot in slot_lists[n]], axis=0),
                 (((1,), (1,)), ((), ())),
                 preferred_element_type=F32,
             )
-            valid = [key_lane < count for count in counts]
-            kept = [
-                jnp.where(valid[j], scores[:, j * block : (j + 1) * block] * scale, NEG_FILL)
+            for n, r, g in jobs
+        ]
+        kept = [
+            [
+                jnp.where(masks[n][j], scores[:, j * block : (j + 1) * block] * scale, NEG_FILL)
                 for j in range(sel)
             ]
-            peak = jnp.max(functools.reduce(jnp.maximum, kept), axis=1, keepdims=True)
-            weights = [jnp.where(valid[j], jnp.exp(kept[j] - peak), 0.0) for j in range(sel)]
-            mass = jnp.sum(functools.reduce(jnp.add, weights), axis=1, keepdims=True)
-            high = [w.astype(BF16) for w in weights]
-            low = [(w - h.astype(F32)).astype(BF16) for w, h in zip(weights, high)]
+            for (n, r, g), scores in zip(jobs, raw)
+        ]
+        peaks = [
+            jnp.max(functools.reduce(jnp.maximum, x), axis=1, keepdims=True) for x in kept
+        ]
+        weights = [
+            [jnp.where(masks[n][j], jnp.exp(x[j] - peak), 0.0) for j in range(sel)]
+            for (n, r, g), x, peak in zip(jobs, kept, peaks)
+        ]
+        masses = [
+            jnp.sum(functools.reduce(jnp.add, x), axis=1, keepdims=True) for x in weights
+        ]
+        outs = []
+        for (n, r, g), x in zip(jobs, weights):
+            high = [w.astype(BF16) for w in x]
+            low = [(w - h.astype(F32)).astype(BF16) for w, h in zip(x, high)]
             both = jnp.concatenate(
                 [jnp.concatenate(high, axis=1), jnp.concatenate(low, axis=1)], axis=0
             )
-            values = jnp.concatenate([vc[slot, g] for slot in slots], axis=0)
-            mixed = jnp.dot(both, values, preferred_element_type=F32)
+            values = jnp.concatenate([vc[slot, g] for slot in slot_lists[n]], axis=0)
+            outs.append(jnp.dot(both, values, preferred_element_type=F32))
+        for (n, r, g), mixed, peak, mass in zip(jobs, outs, peaks, masses):
             mixed = mixed[:queries] + mixed[queries:]
             for s in range(steps):
                 accum[r * steps + s, g] = mixed[s * per_kv : (s + 1) * per_kv]
@@ -281,8 +298,7 @@
 
         def attend_owner(b, stat):
             owner = mem_peer(b + 1)
-            for row in range(own_rows):
-                stat = attend_row(owner * own_rows + row, stat)
+            stat = attend_rows([owner * own_rows + row for row in range(own_rows)], stat)
 
             @pl.when(b < mem_count - 1)
             def _():
@@ -292,7 +308,7 @@
 
         stat = lax.fori_loop(0, mem_count, attend_owner, stat)
     else:
-        stat = lax.fori_loop(0, row_count, attend_row, stat)
+        stat = lax.fori_loop(0, row_count, lambda r, x: attend_rows([r], x), stat)
         for k in range(1, mem_count):
             accum_copy(k, mem_peer(k), mem).start()
     for s in range(steps):

time: 37.3 us -> 34.5 us (0.925)
  Pallas kernels: 35.7 us -> 32.9 us
    pallas_call x1, Pallas kernels: 35.7 us -> 32.9 us  [shards(): pl.pallas_call(functools.partial(layer_kernel, mem_count, head_count, chu...]
where the time goes in v3:
time: 34.5 us; the launch traced here: 34.2 us
  Pallas kernels  32.9 us (95%)
  local copies, waits for them, and re-layouts  1.33 us (4%)
    pallas_call x1, Pallas kernels, shards(): pl.pallas_call(functools.partial(layer_kernel, mem_count, head_count, chu...  32.9 us
    unnamed x1, local copies, waits for them, and re-layouts  1.33 us

profile of v3, /device:TPU:0, one launch (start us, length us, event | category | flops | bytes accessed | tf_op | source)
XLA Modules:
  0.0 34.2 jit_solution(16547687687412225858)
XLA Ops:
  0.0 32.9 %shard_map.109 = bf16[4,2048]{1,0:T(4,128)(2,1)} custom-call(s32[8,24]{1,0:T(8,128)} %page_ref.1, s32[8,8]{1,0:T(8,128)} %attend_ref.1, s32[8]{0:T(128)} %length_ref.1, bf16[4,8192]{1,0:T(4,128)(2,1)} %hidden_ref.1, bf16[2048]{0:T(1024)(128)(2,1)} %gain_ref.1, bf16[2048,2048]{1,0:T(8,128)(2,1)} %wq_hbm.1, bf16[2048,256]{1,0:T(8,128)(2,1)} %wk_hbm.1, ...), custom_call_target="tpu_custom_call" | custom-call | tf_op jit(solution)/shard_map/pallas_call | solution.py:479
  32.9 1.3 %copy.13 = bf16[4,2048]{1,0:T(4,128)(2,1)} copy(bf16[4,2048]{1,0:T(4,128)(2,1)} %shard_map.109) | data formatting | bytes 32768

commit v4 on v3

--- a/solution.py
+++ b/solution.py
@@ -296,17 +296,22 @@
     if own_tokens % steps == 0:
         own_rows = own_tokens // steps
 
-        def attend_owner(b, stat):
-            owner = mem_peer(b + 1)
-            stat = attend_rows([owner * own_rows + row for row in range(own_rows)], stat)
-
-            @pl.when(b < mem_count - 1)
-            def _():
-                accum_copy(b + 1, owner, mem).start()
+        together = 2 if mem_count % 2 == 0 else 1
+
+        def attend_owners(b, stat):
+            first = b * together + 1
+            owners = [mem_peer(first + i) for i in range(together)]
+            rows = [owner * own_rows + row for owner in owners for row in range(own_rows)]
+            stat = attend_rows(rows, stat)
+            for i, owner in enumerate(owners):
+
+                @pl.when(first + i < mem_count)
+                def _():
+                    accum_copy(first + i, owner, mem).start()
 
             return stat
 
-        stat = lax.fori_loop(0, mem_count, attend_owner, stat)
+        stat = lax.fori_loop(0, mem_count // together, attend_owners, stat)
     else:
         stat = lax.fori_loop(0, row_count, lambda r, x: attend_rows([r], x), stat)
         for k in range(1, mem_count):

time: 34.5 us -> 34.1 us (0.988)
  Pallas kernels: 32.9 us -> 32.5 us
    pallas_call x1, Pallas kernels: 32.9 us -> 32.5 us  [shards(): pl.pallas_call(functools.partial(layer_kernel, mem_count, head_count, chu...]
where the time goes in v4:
time: 34.1 us; the launch traced here: 33.8 us
  Pallas kernels  32.5 us (95%)
  local copies, waits for them, and re-layouts  1.33 us (4%)
    pallas_call x1, Pallas kernels, shards(): pl.pallas_call(functools.partial(layer_kernel, mem_count, head_count, chu...  32.5 us
    unnamed x1, local copies, waits for them, and re-layouts  1.33 us

profile of v4, /device:TPU:0, one launch (start us, length us, event | category | flops | bytes accessed | tf_op | source)
XLA Modules:
  0.0 33.8 jit_solution(2208490572846624209)
XLA Ops:
  0.0 32.5 %shard_map.109 = bf16[4,2048]{1,0:T(4,128)(2,1)} custom-call(s32[8,24]{1,0:T(8,128)} %page_ref.1, s32[8,8]{1,0:T(8,128)} %attend_ref.1, s32[8]{0:T(128)} %length_ref.1, bf16[4,8192]{1,0:T(4,128)(2,1)} %hidden_ref.1, bf16[2048]{0:T(1024)(128)(2,1)} %gain_ref.1, bf16[2048,2048]{1,0:T(8,128)(2,1)} %wq_hbm.1, bf16[2048,256]{1,0:T(8,128)(2,1)} %wk_hbm.1, ...), custom_call_target="tpu_custom_call" | custom-call | tf_op jit(solution)/shard_map/pallas_call | solution.py:484
  32.5 1.3 %copy.13 = bf16[4,2048]{1,0:T(4,128)(2,1)} copy(bf16[4,2048]{1,0:T(4,128)(2,1)} %shard_map.109) | data formatting | bytes 32768
